TPU v7x, 128 devices: a whole 4x4x4 slice. The times are simulated.
128 devices in a mesh: seq: 32 (over z, x_lo, y), chan: 4 (over x_hi, core).
Axes of the slice: x: 4 (x_hi: 2, x_lo: 2; x = x_hi * 2 + x_lo), y: 4, z: 4, core: 2. Of those that a mesh axis runs over, the one named last changes fastest.
Arguments:
- tokens: bfloat16 [32768, 512], P('seq', 'chan'), may hold values from -6 to 6
- w_in: bfloat16 [512, 3, 512], P(None, None, 'chan'), may hold values from -0.25 to 0.25
- short_filter: float32 [3, 3, 512], P(None, None, 'chan'), may hold values from -3 to 3
- long_filter: float32 [32768, 512], P('seq', 'chan'), may hold values from -0.03125 to 0.03125
- skip_gain: float32 [512], P('chan'), may hold values from 0.5 to 1.5
- w_out: bfloat16 [512, 512], P('chan'), may hold values from -0.25 to 0.25
Outputs:
- mixed: bfloat16 [32768, 512], P('seq', 'chan')
All inputs are finite; a program needn't handle non-finite values.
Results may differ from a plain program's by a relative error of at most 0.007.
Values may be sent and summed in bfloat16 or wider, within the bound.
No kernel may reach another device: no remote copies, remote signals or barrier semaphores. Data moves between devices by JAX's collectives and lax.ppermute only.
A program may use at most 64 MiB of HBM per device.

v0:
```python
import functools
import math

import jax
import jax.numpy as jnp
import ml_dtypes
import numpy as np
from jax import lax
from jax.experimental import pallas as pl
from jax.experimental.pallas import tpu as pltpu
from jax.sharding import PartitionSpec as P


F32 = jnp.float32
BF16 = jnp.bfloat16
VMEM = pltpu.VMEM

SHARDS = 32
CHANS = 4
ROWS = 1024
WIDTH = 128
GROUP = 4
OUTER = 256
INNER = 128
LENGTH = OUTER * INNER
SIG = GROUP * 8
EDGE = 8


def halves(table):
    high = table.astype(ml_dtypes.bfloat16)
    low = (table - high.astype(np.float64)).astype(ml_dtypes.bfloat16)
    return high, low


@functools.lru_cache(None)
def tables():
    k1 = np.arange(OUTER)[:, None]
    a = np.arange(OUTER)[None, :]
    angle = 2 * math.pi / (4 * OUTER) * (a * (4 * k1 + 1) % (4 * OUTER))
    first = np.concatenate([np.cos(angle), -np.sin(angle)], 0)
    last = np.concatenate([np.cos(angle), -np.sin(angle)], 0).T / LENGTH
    p = np.arange(INNER)
    turn = 2 * math.pi / (4 * LENGTH) * (p[None, :] * (4 * k1 + 1) % (4 * LENGTH))
    twiddle = np.concatenate([np.cos(turn), np.sin(turn)], 1).astype(np.float32)
    phase = 2 * math.pi / INNER * (p[:, None] * p[None, :] % INNER)
    c, s = np.cos(phase), np.sin(phase)
    second = np.block([[c, -s], [s, c]])
    third = np.block([[c, s], [-s, c]])
    return twiddle, halves(first), halves(second), halves(third), halves(last)


def split(value):
    high = value.astype(BF16)
    return high, (value - high.astype(F32)).astype(BF16)


def dot(left, right):
    return jnp.dot(left, right, preferred_element_type=F32)


def dot3(left, right):
    (lh, ll), (rh, rl) = left, right
    return dot(lh, rh) + (dot(lh, rl) + dot(ll, rh))


def load_signal(value):
    wide = value.reshape(SHARDS, GROUP, 8, INNER)
    return jnp.concatenate(
        [wide[:, c].reshape(OUTER, INNER).astype(BF16) for c in range(GROUP)], axis=1
    )


def forward(signal, tw, f_hi, f_lo, s_hi, s_lo):
    first = dot(f_hi[...], signal) + dot(f_lo[...], signal)
    cos, sin = tw[:, :INNER], tw[:, INNER:]
    rows = []
    for c in range(GROUP):
        re = first[:OUTER, c * INNER : (c + 1) * INNER]
        im = first[OUTER:, c * INNER : (c + 1) * INNER]
        rows.append(jnp.concatenate([re * cos + im * sin, im * cos - re * sin], axis=1))
    turned = jnp.concatenate(rows, axis=0)
    return dot3(split(turned), (s_hi[...], s_lo[...]))


def conv_kernel(
    sig, coef, tw, f_hi, f_lo, s_hi, s_lo, t_hi, t_lo, l_hi, l_lo, out, scratch, pairs, shifted
):
    spec = forward(load_signal(sig[:, :SIG, :].astype(F32)), tw, f_hi, f_lo, s_hi, s_lo)
    pairs[...] = sig[:, 2 * SIG :, :].astype(F32).reshape(2 * WIDTH, INNER)
    heads, tails = pairs[pl.ds(0, WIDTH, stride=2), :], pairs[pl.ds(1, WIDTH, stride=2), :]
    shifted[:8, :] = jnp.zeros((8, INNER), F32)
    shifted[8:, :] = tails
    before = shifted[8 - GROUP : 8 - GROUP + WIDTH, :]
    pairs[pl.ds(0, WIDTH, stride=2), :] = before
    out[:, SIG:, :] = pairs[...].reshape(SHARDS, EDGE, INNER).astype(BF16)
    terms = (heads + before) * coef[...]
    short = terms + pltpu.roll(terms, INNER - 2, 1) + pltpu.roll(terms, INNER - 4, 1)
    edge = short * pltpu.roll(short, INNER - 6, 1)
    scratch[...] = sig[:, SIG : 2 * SIG, :].astype(F32).reshape(ROWS, INNER)
    lane = lax.broadcasted_iota(jnp.int32, (WIDTH, INNER), 1)
    opening = scratch[pl.ds(0, WIDTH, stride=8), :]
    scratch[pl.ds(0, WIDTH, stride=8), :] = jnp.where(lane < 2, edge, opening)
    mine = forward(load_signal(scratch[...]), tw, f_hi, f_lo, s_hi, s_lo)
    mr, mi = mine[:, :INNER], mine[:, INNER:]
    hr, hi = spec[:, :INNER], spec[:, INNER:]
    product = jnp.concatenate([mr * hr - mi * hi, mr * hi + mi * hr], axis=1)
    back = dot3(split(product), (t_hi[...], t_lo[...]))
    cos, sin = tw[:, :INNER], tw[:, INNER:]
    res, ims = [], []
    for c in range(GROUP):
        re = back[c * OUTER : (c + 1) * OUTER, :INNER]
        im = back[c * OUTER : (c + 1) * OUTER, INNER:]
        res.append(re * cos - im * sin)
        ims.append(im * cos + re * sin)
    turned = jnp.concatenate(
        [jnp.concatenate(res, axis=1), jnp.concatenate(ims, axis=1)], axis=0
    )
    y = dot3((l_hi[...], l_lo[...]), split(turned))
    parts = [
        y[:, c * INNER : (c + 1) * INNER].reshape(SHARDS, 1, 8, INNER) for c in range(GROUP)
    ]
    wide = jnp.concatenate(parts, axis=1).reshape(SHARDS, GROUP * 8, INNER)
    out[:, :SIG, :] = wide.astype(BF16)


def to_channels(value, scratch):
    for q in range(8):
        scratch[pl.ds(q, WIDTH, stride=8), :] = value[q * INNER : (q + 1) * INNER].T
    return scratch[...].reshape(SHARDS, GROUP * 8, INNER).astype(BF16)


def turn_kernel(value, out, scratch):
    out[...] = to_channels(value[...], scratch)


def project_kernel(
    me, t0, t1, t2, t3, w, short_filter, skip, taps, out, gate, direct, edge, ext, scratch, pairs, square
):
    chan = me[0]
    order = [pl.ds(pl.multiple_of((chan ^ r) * WIDTH, WIDTH), WIDTH) for r in range(CHANS)]
    weights = jnp.concatenate(
        [jnp.concatenate([w[g, rows, :] for rows in order], axis=0) for g in range(3)], axis=1
    )
    tokens = jnp.concatenate([t0[...], t1[...], t2[...], t3[...]], axis=1)
    ext[:8, :] = jnp.zeros((8, 3 * WIDTH), F32)
    ext[8:, :] = dot(tokens, weights).astype(BF16).astype(F32)
    short = []
    for g in range(3):
        lanes = slice(g * WIDTH, (g + 1) * WIDTH)
        tap = [short_filter[j, g, :].reshape(1, WIDTH) for j in range(3)]
        short.append(
            tap[0] * ext[8:, lanes]
            + tap[1] * ext[7 : ROWS + 7, lanes]
            + tap[2] * ext[6 : ROWS + 6, lanes]
        )
    inner = short[0] * short[1]
    gate[...] = short[2]
    direct[...] = skip[...] * inner
    edge[:8, :] = short[0][:8]
    edge[8:, :] = short[1][:8]
    out[:, :SIG, :] = taps[...]
    out[:, SIG : 2 * SIG, :] = to_channels(inner, scratch)
    square[...] = jnp.zeros((INNER, WIDTH), F32)
    for g in range(2):
        lanes = slice(g * WIDTH, (g + 1) * WIDTH)
        square[6 * g : 6 * g + 2, :] = ext[8:10, lanes]
        square[6 * g + 3 : 6 * g + 4, :] = ext[8:9, lanes]
    pairs[pl.ds(0, WIDTH, stride=2), :] = square[...].T
    square[...] = jnp.zeros((INNER, WIDTH), F32)
    for g in range(3):
        lanes = slice(g * WIDTH, (g + 1) * WIDTH)
        square[6 * g + 2 : 6 * g + 3, :] = ext[ROWS + 7 : ROWS + 8, lanes]
        square[6 * g + 4 : 6 * g + 6, :] = ext[ROWS + 6 : ROWS + 8, lanes]
    pairs[pl.ds(1, WIDTH, stride=2), :] = square[...].T
    out[:, 2 * SIG :, :] = pairs[...].reshape(SHARDS, EDGE, INNER).astype(BF16)


def gate_kernel(conv, gate, direct, edge, short_filter, skip, out, scratch, pairs, square):
    scratch[...] = conv[:, :SIG, :].astype(F32).reshape(ROWS, WIDTH)
    pairs[...] = conv[:, SIG:, :].astype(F32).reshape(2 * WIDTH, INNER)
    square[...] = pairs[pl.ds(0, WIDTH, stride=2), :].T
    short = []
    for g, start in enumerate((edge[:2, :], edge[8:10, :], gate[:2, :])):
        tap = [short_filter[j, g, :].reshape(1, WIDTH) for j in range(3)]
        short.append(
            start + tap[1] * square[6 * g + 2 : 6 * g + 4, :] + tap[2] * square[6 * g + 4 : 6 * g + 6, :]
        )
    inner = short[0] * short[1]
    for q in range(8):
        rows = slice(q * INNER, (q + 1) * INNER)
        back = scratch[pl.ds(q, WIDTH, stride=8), :].T
        out[rows, :] = (gate[rows, :] * (back + direct[rows, :])).astype(BF16)
        if q == 0:
            gates = jnp.concatenate([short[2], gate[2:16, :]], axis=0)
            directs = jnp.concatenate([skip[...] * inner, direct[2:16, :]], axis=0)
            out[:16, :] = (gates * (back[:16] + directs)).astype(BF16)


def output_kernel(g0, g1, g2, g3, w0, w1, w2, w3, out):
    gated = jnp.concatenate([g0[...], g1[...], g2[...], g3[...]], axis=1)
    weights = jnp.concatenate([w0[...], w1[...], w2[...], w3[...]], axis=0)
    out[...] = dot(gated, weights).astype(BF16)


def call(kernel, out_shape, args, scratch=(), smem=0, flops=0, vmem=16):
    many = isinstance(out_shape, (list, tuple))
    specs = [pl.BlockSpec(memory_space=pltpu.SMEM)] * smem
    specs += [pl.BlockSpec(memory_space=VMEM)] * (len(args) - smem)
    outs = [pl.BlockSpec(memory_space=VMEM) for _ in out_shape] if many else pl.BlockSpec(memory_space=VMEM)
    moved = sum(x.size * x.dtype.itemsize for x in args)
    return pl.pallas_call(
        kernel,
        out_shape=out_shape,
        in_specs=specs,
        out_specs=outs,
        scratch_shapes=list(scratch),
        cost_estimate=pl.CostEstimate(flops=flops, bytes_accessed=moved, transcendentals=0),
        compiler_params=pltpu.CompilerParams(vmem_limit_bytes=vmem << 20),
    )(*args)


def swap(value, distance):
    return lax.ppermute(value, "chan", [(i, i ^ distance) for i in range(CHANS)])


def operator(tokens, w_in, short_filter, long_filter, skip_gain, w_out):
    chan = lax.axis_index("chan")
    shard = lax.axis_index("seq")
    me = jnp.stack([chan, shard]).astype(jnp.int32)
    turned = VMEM((ROWS, WIDTH), F32)
    pairs, square = VMEM((2 * WIDTH, INNER), F32), VMEM((INNER, WIDTH), F32)
    block = jax.ShapeDtypeStruct((ROWS, WIDTH), F32)

    tw, first, second, third, last = tables()
    tw = jnp.asarray(tw)
    first, second, third, last = [tuple(jnp.asarray(x) for x in t) for t in (first, second, third, last)]

    beyond = swap(tokens, 2)
    near = swap(tokens, 1)
    near, w_out, own_filter = lax.optimization_barrier((near, w_out, short_filter))
    pieces = [lax.dynamic_slice_in_dim(w_out, (chan ^ r) * WIDTH, WIDTH, axis=1) for r in range(CHANS)]
    columns = [pieces[0], swap(pieces[1], 1)]
    over = jnp.concatenate([pieces[2], pieces[3]], axis=0)
    coef = lax.dynamic_slice_in_dim(own_filter, shard * GROUP, GROUP, axis=2)[:, :2, :]
    coef = jnp.repeat(coef.transpose(2, 1, 0).reshape(GROUP, 6), 2, axis=1)
    coef = jnp.tile(jnp.pad(coef, ((0, 0), (0, INNER - 12))), (SHARDS, 1))
    weights = w_in.transpose(1, 0, 2)
    taps = call(
        turn_kernel, jax.ShapeDtypeStruct((SHARDS, SIG, INNER), BF16), [long_filter], [turned]
    )
    beyond, taps, weights, columns, near, coef, over = lax.optimization_barrier(
        (beyond, taps, weights, columns, near, coef, over)
    )
    far = swap(beyond, 1)
    over = swap(over, 2)

    skip = skip_gain.reshape(1, WIDTH)
    inner, gate, direct, edge = call(
        project_kernel,
        [
            jax.ShapeDtypeStruct((SHARDS, 2 * SIG + EDGE, INNER), BF16),
            block,
            block,
            jax.ShapeDtypeStruct((16, WIDTH), F32),
        ],
        [me, tokens, near, beyond, far, weights, short_filter, skip, taps],
        [VMEM((ROWS + 8, 3 * WIDTH), F32), turned, pairs, square],
        smem=1,
        flops=2 * 200 << 20,
    )
    inner = lax.all_to_all(inner, "seq", 0, 0)
    conv = call(
        conv_kernel,
        jax.ShapeDtypeStruct((SHARDS, SIG + EDGE, INNER), BF16),
        [inner, coef, tw, *first, *second, *third, *last],
        [turned, pairs, VMEM((WIDTH + 8, INNER), F32)],
        flops=2 * 1060 << 20,
        vmem=32,
    )
    conv = lax.all_to_all(conv, "seq", 0, 0)
    gated = call(
        gate_kernel,
        jax.ShapeDtypeStruct((ROWS, WIDTH), BF16),
        [conv, gate, direct, edge, short_filter, skip],
        [turned, pairs, square],
    )
    beyond = swap(gated, 2)
    near = swap(gated, 1)
    over, near = lax.optimization_barrier((over, near))
    last_column = swap(over[WIDTH:], 1)
    beyond, last_column = lax.optimization_barrier((beyond, last_column))
    columns += [over[:WIDTH], last_column]
    return call(
        output_kernel,
        jax.ShapeDtypeStruct((ROWS, WIDTH), BF16),
        [gated, near, beyond, swap(beyond, 1), *columns],
        flops=2 * 64 << 20,
    )


def solution(mesh):
    return jax.shard_map(
        operator,
        mesh=mesh,
        in_specs=(
            P("seq", "chan"),
            P(None, None, "chan"),
            P(None, None, "chan"),
            P("seq", "chan"),
            P("chan"),
            P("chan", None),
        ),
        out_specs=P("seq", "chan"),
        check_vma=False,
    )
```

profile of v0, /device:TPU:1, one launch (start us, length us, event | category | flops | bytes accessed | tf_op | source)
XLA Modules:
  0.0 69.6 jit_solution(8879924383309034736)
XLA Ops:
  0.0 1.4 %collective-permute-start.1 = (bf16[1024,128]{1,0:T(8,128)(2,1)}, bf16[1024,128]{1,0:T(8,128)(2,1)S(1)}, u32[]{:S(2)}, u32[]{:S(2)}) collective-permute-start(bf16[1024,128]{1,0:T(8,128)(2,1)} %t0.1), channel_id=1, source_target_pairs={{0,1},{1,0},{2,3},{3,2},{4,5},{5,4},{6,7},{7,6},{8,9},{9,8},{10,11... | collective-permute-start | bytes 786440 | tf_op jit(solution)/shard_map/ppermute | solution.py:224
  1.4 2.9 %collective-permute-start = (bf16[1024,128]{1,0:T(8,128)(2,1)}, bf16[1024,128]{1,0:T(8,128)(2,1)S(1)}, u32[]{:S(2)}, u32[]{:S(2)}) collective-permute-start(bf16[1024,128]{1,0:T(8,128)(2,1)} %t0.1), channel_id=1, source_target_pairs={{0,2},{1,3},{2,0},{3,1},{4,6},{5,7},{6,4},{7,5},{8,10},{9,11},{10,... | collective-permute-start | bytes 786440 | tf_op jit(solution)/shard_map/ppermute | solution.py:224
  4.2 1.0 %copy-done = f32[1024,128]{1,0:T(8,128)S(1)} copy-done((f32[1024,128]{1,0:T(8,128)S(1)}, f32[1024,128]{1,0:T(8,128)}, u32[]{:S(2)}) %copy-start) | copy-done | bytes 524312
  5.3 0.2 shard_map.145.taps
  5.5 0.0 copy-start.1
  5.5 0.0 collective-permute-done.1.t1
  5.6 0.6 copy-done.14
  6.2 0.4 collective-permute-start.2
  6.6 0.7 copy-done.3
  7.3 0.1 dynamic-slice_bitcast_fusion
  7.4 0.1 copy.24
  7.5 3.5 %collective-permute-done.t2 = bf16[1024,128]{1,0:T(8,128)(2,1)S(1)} collective-permute-done((bf16[1024,128]{1,0:T(8,128)(2,1)}, bf16[1024,128]{1,0:T(8,128)(2,1)S(1)}, u32[]{:S(2)}, u32[]{:S(2)}) %collective-permute-start) | collective-permute-done | bytes 262176 | tf_op jit(solution)/shard_map/ppermute | solution.py:224
  11.0 0.0 collective-permute-done.2.w1
  11.0 0.9 %collective-permute-start.3 = (bf16[1024,128]{1,0:T(8,128)(2,1)S(1)}, bf16[1024,128]{1,0:T(8,128)(2,1)S(1)}, u32[]{:S(2)}, u32[]{:S(2)}) collective-permute-start(bf16[1024,128]{1,0:T(8,128)(2,1)S(1)} %collective-permute-done.t2), channel_id=1, source_target_pairs={{0,1},{1,0},{2,3},{3,2},{4,5},{5,4},{6,7},{7,6},{8,9},{9,8},{10,11... | collective-permute-start | bytes 786440 | tf_op jit(solution)/shard_map/ppermute | solution.py:224
  11.9 0.1 pad_add_fusion.me
  12.0 1.1 %collective-permute-done.3.t3 = bf16[1024,128]{1,0:T(8,128)(2,1)S(1)} collective-permute-done((bf16[1024,128]{1,0:T(8,128)(2,1)S(1)}, bf16[1024,128]{1,0:T(8,128)(2,1)S(1)}, u32[]{:S(2)}, u32[]{:S(2)}) %collective-permute-start.3) | collective-permute-done | bytes 262176 | tf_op jit(solution)/shard_map/ppermute | solution.py:224
  13.1 0.0 copy-done.2
  13.1 0.0 copy-done.1
  13.1 0.0 copy-done.4
  13.1 0.0 copy-start.11
  13.1 0.0 copy-start.12
  13.1 0.0 copy-start.13
  13.1 1.7 %shard_map.146 = (bf16[32,72,128]{2,1,0:T(8,128)(2,1)S(1)}, f32[1024,128]{1,0:T(8,128)S(1)}, f32[1024,128]{1,0:T(8,128)S(1)}, f32[16,128]{1,0:T(8,128)S(1)}) custom-call(s32[2]{0:T(128)S(1)} %pad_add_fusion.me, bf16[1024,128]{1,0:T(8,128)(2,1)S(1)} %copy-done.2, bf16[1024,128]{1,0:T(8,128)(2,1)S(1)} %collective-permute-done.1.t1, ...), custom_call_target="tpu_custom_call" | custom-call | flops 419430400 | bytes 1709064 | tf_op jit(solution)/shard_map/pallas_call | solution.py:212
  14.8 0.0 copy-start.5
  14.9 0.0 copy-start.6
  14.9 0.0 copy-start.7
  14.9 0.0 copy-start.8
  14.9 0.0 copy-start.10
  14.9 19.9 %all_to_all.10.sig = bf16[32,72,128]{2,1,0:T(8,128)(2,1)S(1)} all-to-all(bf16[32,72,128]{2,1,0:T(8,128)(2,1)S(1)} %get-tuple-element.31), channel_id=1, replica_groups=mesh['seq'=32,'chan'=4] {'seq'}, dimensions={0} | all-to-all | bytes 1179648 | tf_op jit(solution)/shard_map/all_to_all | solution.py:272
  34.8 0.0 copy-done.9
  34.8 0.0 copy-done.11
  34.8 0.0 copy-done.12
  34.8 0.0 copy-done.13
  34.8 0.0 copy-done.5
  34.9 3.3 %shard_map.147 = bf16[32,40,128]{2,1,0:T(8,128)(2,1)S(1)} custom-call(bf16[32,72,128]{2,1,0:T(8,128)(2,1)S(1)} %all_to_all.10.sig, f32[128,128]{1,0:T(8,128)S(1)} %bitcast.12, f32[256,256]{1,0:T(8,128)S(1)} %copy-done.9, bf16[512,256]{1,0:T(8,128)(2,1)S(1)} %copy-done.8, bf16[512,256]{1,0:T(8,128)(2,1)S(1)} %copy-done.7, bf16[256,256]{1,0:T(8,128)(2,1)S(1)} %copy-done.13, ...), custom_call_target="tpu_custom_call" | custom-call | flops 2222981120 | bytes 2490368 | tf_op jit(solution)/shard_map/pallas_call | solution.py:212
  38.2 13.6 %all_to_all.11.conv = bf16[32,40,128]{2,1,0:T(8,128)(2,1)S(1)} all-to-all(bf16[32,40,128]{2,1,0:T(8,128)(2,1)S(1)} %shard_map.147), channel_id=1, replica_groups=mesh['seq'=32,'chan'=4] {'seq'}, dimensions={0} | all-to-all | bytes 655360 | tf_op jit(solution)/shard_map/all_to_all | solution.py:281
  51.8 0.3 shard_map.148.g0
  52.1 2.5 %collective-permute-start.5 = (bf16[1024,128]{1,0:T(8,128)(2,1)S(1)}, bf16[1024,128]{1,0:T(8,128)(2,1)S(1)}, u32[]{:S(2)}, u32[]{:S(2)}) collective-permute-start(bf16[1024,128]{1,0:T(8,128)(2,1)S(1)} %shard_map.148.g0), channel_id=1, source_target_pairs={{0,1},{1,0},{2,3},{3,2},{4,5},{5,4},{6,7},{7,6},{8,9},{9,8},{10,11... | collective-permute-start | bytes 786440 | tf_op jit(solution)/shard_map/ppermute | solution.py:224
  54.6 2.4 %collective-permute-start.4 = (bf16[256,128]{1,0:T(8,128)(2,1)S(1)}, bf16[256,128]{1,0:T(8,128)(2,1)S(1)}, u32[]{:S(2)}, u32[]{:S(2)}) collective-permute-start(bf16[256,128]{1,0:T(8,128)(2,1)S(1)} %pad_maximum_fusion), channel_id=1, source_target_pairs={{0,2},{1,3},{2,0},{3,1},{4,6},{5,7},{6,4},{7,5},{8,10},{9,11},{10,... | collective-permute-start | bytes 196616 | tf_op jit(solution)/shard_map/ppermute | solution.py:224
  57.0 0.5 collective-permute-start.6
  57.6 2.1 %collective-permute-done.4 = bf16[256,128]{1,0:T(8,128)(2,1)S(1)} collective-permute-done((bf16[256,128]{1,0:T(8,128)(2,1)S(1)}, bf16[256,128]{1,0:T(8,128)(2,1)S(1)}, u32[]{:S(2)}, u32[]{:S(2)}) %collective-permute-start.4) | collective-permute-done | bytes 65568 | tf_op jit(solution)/shard_map/ppermute | solution.py:224
  59.6 0.0 collective-permute-done.5.g1
  59.7 1.0 %collective-permute-start.7 = (bf16[128,128]{1,0:T(8,128)(2,1)S(1)}, bf16[128,128]{1,0:T(8,128)(2,1)S(1)}, u32[]{:S(2)}, u32[]{:S(2)}) collective-permute-start(bf16[128,128]{1,0:T(8,128)(2,1)S(1)} %get-tuple-element.48), channel_id=1, source_target_pairs={{0,1},{1,0},{2,3},{3,2},{4,5},{5,4},{6,7},{7,6},{8,9},{9,8},{10,11... | collective-permute-start | bytes 98312 | tf_op jit(solution)/shard_map/ppermute | solution.py:224
  60.7 5.3 %collective-permute-done.6.g2 = bf16[1024,128]{1,0:T(8,128)(2,1)S(1)} collective-permute-done((bf16[1024,128]{1,0:T(8,128)(2,1)S(1)}, bf16[1024,128]{1,0:T(8,128)(2,1)S(1)}, u32[]{:S(2)}, u32[]{:S(2)}) %collective-permute-start.6) | collective-permute-done | bytes 262176 | tf_op jit(solution)/shard_map/ppermute | solution.py:224
  66.0 0.0 collective-permute-done.7.w3
  66.0 1.2 %collective-permute-start.8 = (bf16[1024,128]{1,0:T(8,128)(2,1)S(1)}, bf16[1024,128]{1,0:T(8,128)(2,1)S(1)}, u32[]{:S(2)}, u32[]{:S(2)}) collective-permute-start(bf16[1024,128]{1,0:T(8,128)(2,1)S(1)} %collective-permute-done.6.g2), channel_id=1, source_target_pairs={{0,1},{1,0},{2,3},{3,2},{4,5},{5,4},{6,7},{7,6},{8,9},{9,8},{10,11... | collective-permute-start | bytes 786440 | tf_op jit(solution)/shard_map/ppermute | solution.py:224
  67.3 1.2 %collective-permute-done.8.g3 = bf16[1024,128]{1,0:T(8,128)(2,1)S(1)} collective-permute-done((bf16[1024,128]{1,0:T(8,128)(2,1)S(1)}, bf16[1024,128]{1,0:T(8,128)(2,1)S(1)}, u32[]{:S(2)}, u32[]{:S(2)}) %collective-permute-start.8) | collective-permute-done | bytes 262176 | tf_op jit(solution)/shard_map/ppermute | solution.py:224
  68.4 1.1 %shard_map.149 = bf16[1024,128]{1,0:T(8,128)(2,1)} custom-call(bf16[1024,128]{1,0:T(8,128)(2,1)S(1)} %shard_map.148.g0, bf16[1024,128]{1,0:T(8,128)(2,1)S(1)} %collective-permute-done.5.g1, bf16[1024,128]{1,0:T(8,128)(2,1)S(1)} %collective-permute-done.6.g2, bf16[1024,128]{1,0:T(8,128)(2,1)S(1)} %collective-permute-done.8.g3, ...), custom_call_target="tpu_custom_call" | custom-call | flops 134217728 | bytes 1179648 | tf_op jit(solution)/shard_map/pallas_call | solution.py:212
  (19 shorter events, 0.1 us)
Async XLA Ops:
  0.0 5.5 %collective-permute-start.1 = (bf16[1024,128]{1,0:T(8,128)(2,1)}, bf16[1024,128]{1,0:T(8,128)(2,1)S(1)}, u32[]{:S(2)}, u32[]{:S(2)}) collective-permute-start(bf16[1024,128]{1,0:T(8,128)(2,1)} %t0.1), channel_id=1, source_target_pairs={{0,1},{1,0},{2,3},{3,2},{4,5},{5,4},{6,7},{7,6},{8,9},{9,8},{10,11... | collective-permute-start | bytes 786440 | tf_op jit(solution)/shard_map/ppermute | solution.py:224
  1.4 9.6 %collective-permute-start = (bf16[1024,128]{1,0:T(8,128)(2,1)}, bf16[1024,128]{1,0:T(8,128)(2,1)S(1)}, u32[]{:S(2)}, u32[]{:S(2)}) collective-permute-start(bf16[1024,128]{1,0:T(8,128)(2,1)} %t0.1), channel_id=1, source_target_pairs={{0,2},{1,3},{2,0},{3,1},{4,6},{5,7},{6,4},{7,5},{8,10},{9,11},{10,... | collective-permute-start | bytes 786440 | tf_op jit(solution)/shard_map/ppermute | solution.py:224
  4.2 1.0 %copy-start = (f32[1024,128]{1,0:T(8,128)S(1)}, f32[1024,128]{1,0:T(8,128)}, u32[]{:S(2)}) copy-start(f32[1024,128]{1,0:T(8,128)} %value.1) | copy-start | bytes 1572868
  5.3 0.9 %copy-start.14 = (bf16[128,512]{1,0:T(8,128)(2,1)S(1)}, bf16[128,512]{1,0:T(8,128)(2,1)}, u32[]{:S(2)}) copy-start(bf16[128,512]{1,0:T(8,128)(2,1)} %param.20) | copy-start | bytes 393220
  5.3 7.8 %copy-start.2 = (bf16[1024,128]{1,0:T(8,128)(2,1)S(1)}, bf16[1024,128]{1,0:T(8,128)(2,1)}, u32[]{:S(2)}) copy-start(bf16[1024,128]{1,0:T(8,128)(2,1)} %t0.1) | copy-start | bytes 786436
  5.5 7.6 %copy-start.1 = (bf16[512,3,128]{2,0,1:T(8,128)(2,1)S(1)}, bf16[512,3,128]{2,0,1:T(8,128)(2,1)}, u32[]{:S(2)}) copy-start(bf16[512,3,128]{2,0,1:T(8,128)(2,1)} %param.16) | copy-start | bytes 1179652
  6.2 4.7 %collective-permute-start.2 = (bf16[128,128]{1,0:T(8,128)(2,1)S(1)}, bf16[128,128]{1,0:T(8,128)(2,1)S(1)}, u32[]{:S(2)}, u32[]{:S(2)}) collective-permute-start(bf16[128,128]{1,0:T(8,128)(2,1)S(1)} %get-tuple-element.45), channel_id=1, source_target_pairs={{0,1},{1,0},{2,3},{3,2},{4,5},{5,4},{6,7},{7,6},{8,9},{9,8},{10,11... | collective-permute-start | bytes 98312 | tf_op jit(solution)/shard_map/ppermute | solution.py:224
  6.6 0.7 copy-start.3
  11.0 2.1 %collective-permute-start.3 = (bf16[1024,128]{1,0:T(8,128)(2,1)S(1)}, bf16[1024,128]{1,0:T(8,128)(2,1)S(1)}, u32[]{:S(2)}, u32[]{:S(2)}) collective-permute-start(bf16[1024,128]{1,0:T(8,128)(2,1)S(1)} %collective-permute-done.t2), channel_id=1, source_target_pairs={{0,1},{1,0},{2,3},{3,2},{4,5},{5,4},{6,7},{7,6},{8,9},{9,8},{10,11... | collective-permute-start | bytes 786440 | tf_op jit(solution)/shard_map/ppermute | solution.py:224
  12.0 1.1 %copy-start.4 = (f32[128]{0:T(128)S(1)}, f32[128]{0:T(128)}, u32[]{:S(2)}) copy-start(f32[128]{0:T(128)} %param.19) | copy-start | bytes 1540
  13.1 21.7 %copy-start.9 = (f32[256,256]{1,0:T(8,128)S(1)}, f32[256,256]{1,0:T(8,128)}, u32[]{:S(2)}) copy-start(f32[256,256]{1,0:T(8,128)} %constant.43.clone.tw) | copy-start | bytes 786436
  13.1 21.7 %copy-start.11 = (bf16[256,256]{1,0:T(8,128)(2,1)S(1)}, bf16[256,256]{1,0:T(8,128)(2,1)}, u32[]{:S(2)}) copy-start(bf16[256,256]{1,0:T(8,128)(2,1)} %constant.48.clone.t_hi) | copy-start | bytes 393220
  13.1 21.7 %copy-start.12 = (bf16[256,256]{1,0:T(8,128)(2,1)S(1)}, bf16[256,256]{1,0:T(8,128)(2,1)}, u32[]{:S(2)}) copy-start(bf16[256,256]{1,0:T(8,128)(2,1)} %constant.47.clone.s_lo) | copy-start | bytes 393220
  13.1 21.7 %copy-start.13 = (bf16[256,256]{1,0:T(8,128)(2,1)S(1)}, bf16[256,256]{1,0:T(8,128)(2,1)}, u32[]{:S(2)}) copy-start(bf16[256,256]{1,0:T(8,128)(2,1)} %constant.46.clone.s_hi) | copy-start | bytes 393220
  14.8 20.0 %copy-start.5 = (bf16[256,512]{1,0:T(8,128)(2,1)S(1)}, bf16[256,512]{1,0:T(8,128)(2,1)}, u32[]{:S(2)}) copy-start(bf16[256,512]{1,0:T(8,128)(2,1)} %constant.51.clone.l_lo) | copy-start | bytes 786436
  14.9 20.0 %copy-start.6 = (bf16[256,512]{1,0:T(8,128)(2,1)S(1)}, bf16[256,512]{1,0:T(8,128)(2,1)}, u32[]{:S(2)}) copy-start(bf16[256,512]{1,0:T(8,128)(2,1)} %constant.50.clone.l_hi) | copy-start | bytes 786436
  14.9 20.0 %copy-start.7 = (bf16[512,256]{1,0:T(8,128)(2,1)S(1)}, bf16[512,256]{1,0:T(8,128)(2,1)}, u32[]{:S(2)}) copy-start(bf16[512,256]{1,0:T(8,128)(2,1)} %constant.45.clone.f_lo) | copy-start | bytes 786436
  14.9 20.0 %copy-start.8 = (bf16[512,256]{1,0:T(8,128)(2,1)S(1)}, bf16[512,256]{1,0:T(8,128)(2,1)}, u32[]{:S(2)}) copy-start(bf16[512,256]{1,0:T(8,128)(2,1)} %constant.44.clone.f_hi) | copy-start | bytes 786436
  14.9 20.0 %copy-start.10 = (bf16[256,256]{1,0:T(8,128)(2,1)S(1)}, bf16[256,256]{1,0:T(8,128)(2,1)}, u32[]{:S(2)}) copy-start(bf16[256,256]{1,0:T(8,128)(2,1)} %constant.49.clone.t_lo) | copy-start | bytes 393220
  52.1 7.6 %collective-permute-start.5 = (bf16[1024,128]{1,0:T(8,128)(2,1)S(1)}, bf16[1024,128]{1,0:T(8,128)(2,1)S(1)}, u32[]{:S(2)}, u32[]{:S(2)}) collective-permute-start(bf16[1024,128]{1,0:T(8,128)(2,1)S(1)} %shard_map.148.g0), channel_id=1, source_target_pairs={{0,1},{1,0},{2,3},{3,2},{4,5},{5,4},{6,7},{7,6},{8,9},{9,8},{10,11... | collective-permute-start | bytes 786440 | tf_op jit(solution)/shard_map/ppermute | solution.py:224
  54.6 5.1 %collective-permute-start.4 = (bf16[256,128]{1,0:T(8,128)(2,1)S(1)}, bf16[256,128]{1,0:T(8,128)(2,1)S(1)}, u32[]{:S(2)}, u32[]{:S(2)}) collective-permute-start(bf16[256,128]{1,0:T(8,128)(2,1)S(1)} %pad_maximum_fusion), channel_id=1, source_target_pairs={{0,2},{1,3},{2,0},{3,1},{4,6},{5,7},{6,4},{7,5},{8,10},{9,11},{10,... | collective-permute-start | bytes 196616 | tf_op jit(solution)/shard_map/ppermute | solution.py:224
  57.0 9.0 %collective-permute-start.6 = (bf16[1024,128]{1,0:T(8,128)(2,1)S(1)}, bf16[1024,128]{1,0:T(8,128)(2,1)S(1)}, u32[]{:S(2)}, u32[]{:S(2)}) collective-permute-start(bf16[1024,128]{1,0:T(8,128)(2,1)S(1)} %shard_map.148.g0), channel_id=1, source_target_pairs={{0,2},{1,3},{2,0},{3,1},{4,6},{5,7},{6,4},{7,5},{8,10},{9,11},{10,... | collective-permute-start | bytes 786440 | tf_op jit(solution)/shard_map/ppermute | solution.py:224
  59.7 6.4 %collective-permute-start.7 = (bf16[128,128]{1,0:T(8,128)(2,1)S(1)}, bf16[128,128]{1,0:T(8,128)(2,1)S(1)}, u32[]{:S(2)}, u32[]{:S(2)}) collective-permute-start(bf16[128,128]{1,0:T(8,128)(2,1)S(1)} %get-tuple-element.48), channel_id=1, source_target_pairs={{0,1},{1,0},{2,3},{3,2},{4,5},{5,4},{6,7},{7,6},{8,9},{9,8},{10,11... | collective-permute-start | bytes 98312 | tf_op jit(solution)/shard_map/ppermute | solution.py:224
  66.0 2.4 %collective-permute-start.8 = (bf16[1024,128]{1,0:T(8,128)(2,1)S(1)}, bf16[1024,128]{1,0:T(8,128)(2,1)S(1)}, u32[]{:S(2)}, u32[]{:S(2)}) collective-permute-start(bf16[1024,128]{1,0:T(8,128)(2,1)S(1)} %collective-permute-done.6.g2), channel_id=1, source_target_pairs={{0,1},{1,0},{2,3},{3,2},{4,5},{5,4},{6,7},{7,6},{8,9},{9,8},{10,11... | collective-permute-start | bytes 786440 | tf_op jit(solution)/shard_map/ppermute | solution.py:224
where the time goes:
time: 69.8 us; the launch traced here: 69.6 us
  blocking collectives  33.5 us (48%)
  starting transfers between devices  13.3 us (19%)
  waiting for transfers between devices  13.2 us (19%)
  Pallas kernels  6.66 us (10%)
  local copies, waits for them, and re-layouts  2.68 us (4%)
    all_to_all x1, blocking collectives, operator(): inner = lax.all_to_all(inner, 'seq', 0, 0)  19.9 us
    all_to_all x1, blocking collectives, operator(): conv = lax.all_to_all(conv, 'seq', 0, 0)  13.6 us
    ppermute x9, starting transfers between devices, swap(): lax.ppermute(value, 'chan', [(i, i ^ distance) for i in range(CHANS)])  13.3 us
    ppermute x9, waiting for transfers between devices, swap(): lax.ppermute(value, 'chan', [(i, i ^ distance) for i in range(CHANS)])  13.2 us
    pallas_call x5, Pallas kernels, call(): pl.pallas_call(kernel, out_shape=out_shape, in_specs=specs, out_specs=out...  6.66 us
    unnamed x31, local copies, waits for them, and re-layouts  2.52 us
  transfers between devices with their start and end apart: 9, of which 5 were waited for; matrix products, arithmetic and copies ran while one was open for 0% of the time, Pallas kernels for 0%

commit v1 on v0

--- a/solution.py
+++ b/solution.py
@@ -24,6 +24,7 @@
 INNER = 128
 LENGTH = OUTER * INNER
 SIG = GROUP * 8
+PARTS = 4
 EDGE = 8
 
 
@@ -61,7 +62,7 @@
 
 def dot3(left, right):
     (lh, ll), (rh, rl) = left, right
-    return dot(lh, rh) + (dot(lh, rl) + dot(ll, rh))
+    return dot(jnp.concatenate([lh, lh, ll], axis=1), jnp.concatenate([rl, rh, rh], axis=0))
 
 
 def load_signal(value):
@@ -72,7 +73,9 @@
 
 
 def forward(signal, tw, f_hi, f_lo, s_hi, s_lo):
-    first = dot(f_hi[...], signal) + dot(f_lo[...], signal)
+    first = dot(
+        jnp.concatenate([f_lo[...], f_hi[...]], axis=1), jnp.concatenate([signal, signal], axis=0)
+    )
     cos, sin = tw[:, :INNER], tw[:, INNER:]
     rows = []
     for c in range(GROUP):
@@ -197,17 +200,24 @@
             out[:16, :] = (gates * (back[:16] + directs)).astype(BF16)
 
 
-def output_kernel(g0, g1, g2, g3, w0, w1, w2, w3, out):
-    gated = jnp.concatenate([g0[...], g1[...], g2[...], g3[...]], axis=1)
+def output_kernel(g0, g1, g2, g3, w0, w1, w2, w3, out, held, sems):
     weights = jnp.concatenate([w0[...], w1[...], w2[...], w3[...]], axis=0)
-    out[...] = dot(gated, weights).astype(BF16)
-
-
-def call(kernel, out_shape, args, scratch=(), smem=0, flops=0, vmem=16):
+    copies = []
+    for part in range(PARTS):
+        rows = slice(part * ROWS // PARTS, (part + 1) * ROWS // PARTS)
+        gated = jnp.concatenate([g[rows, :] for g in (g0, g1, g2, g3)], axis=1)
+        held[rows, :] = dot(gated, weights).astype(BF16)
+        copies.append(pltpu.make_async_copy(held.at[rows], out.at[rows], sems.at[part]))
+        copies[-1].start()
+    for copy in copies:
+        copy.wait()
+
+
+def call(kernel, out_shape, args, scratch=(), smem=0, flops=0, vmem=16, out_space=VMEM):
     many = isinstance(out_shape, (list, tuple))
     specs = [pl.BlockSpec(memory_space=pltpu.SMEM)] * smem
     specs += [pl.BlockSpec(memory_space=VMEM)] * (len(args) - smem)
-    outs = [pl.BlockSpec(memory_space=VMEM) for _ in out_shape] if many else pl.BlockSpec(memory_space=VMEM)
+    outs = [pl.BlockSpec(memory_space=VMEM) for _ in out_shape] if many else pl.BlockSpec(memory_space=out_space)
     moved = sum(x.size * x.dtype.itemsize for x in args)
     return pl.pallas_call(
         kernel,
@@ -295,6 +305,8 @@
         output_kernel,
         jax.ShapeDtypeStruct((ROWS, WIDTH), BF16),
         [gated, near, beyond, swap(beyond, 1), *columns],
+        [VMEM((ROWS, WIDTH), BF16), pltpu.SemaphoreType.DMA((PARTS,))],
+        out_space=pl.ANY,
         flops=2 * 64 << 20,
     )
 

time: 69.8 us -> 69.8 us (level)
  no operation moved by 1% of the time
where the time goes in v1:
time: 69.8 us; the launch traced here: 69.5 us
  blocking collectives  33.5 us (48%)
  starting transfers between devices  13.3 us (19%)
  waiting for transfers between devices  13.2 us (19%)
  Pallas kernels  6.59 us (9%)
  local copies, waits for them, and re-layouts  2.68 us (4%)
    all_to_all x1, blocking collectives, operator(): inner = lax.all_to_all(inner, 'seq', 0, 0)  19.9 us
    all_to_all x1, blocking collectives, operator(): conv = lax.all_to_all(conv, 'seq', 0, 0)  13.6 us
    ppermute x9, starting transfers between devices, swap(): lax.ppermute(value, 'chan', [(i, i ^ distance) for i in range(CHANS)])  13.3 us
    ppermute x9, waiting for transfers between devices, swap(): lax.ppermute(value, 'chan', [(i, i ^ distance) for i in range(CHANS)])  13.2 us
    pallas_call x5, Pallas kernels, call(): pl.pallas_call(kernel, out_shape=out_shape, in_specs=specs, out_specs=out...  6.59 us
    unnamed x31, local copies, waits for them, and re-layouts  2.52 us
  transfers between devices with their start and end apart: 9, of which 5 were waited for; matrix products, arithmetic and copies ran while one was open for 0% of the time, Pallas kernels for 0%

profile of v1, /device:TPU:1, one launch (start us, length us, event | category | flops | bytes accessed | tf_op | source)
XLA Modules:
  0.0 69.5 jit_solution(11164573342486891022)
XLA Ops:
  0.0 1.4 %collective-permute-start.1 = (bf16[1024,128]{1,0:T(8,128)(2,1)}, bf16[1024,128]{1,0:T(8,128)(2,1)S(1)}, u32[]{:S(2)}, u32[]{:S(2)}) collective-permute-start(bf16[1024,128]{1,0:T(8,128)(2,1)} %t0.1), channel_id=1, source_target_pairs={{0,1},{1,0},{2,3},{3,2},{4,5},{5,4},{6,7},{7,6},{8,9},{9,8},{10,11... | collective-permute-start | bytes 786440 | tf_op jit(solution)/shard_map/ppermute | solution.py:234
  1.4 2.9 %collective-permute-start = (bf16[1024,128]{1,0:T(8,128)(2,1)}, bf16[1024,128]{1,0:T(8,128)(2,1)S(1)}, u32[]{:S(2)}, u32[]{:S(2)}) collective-permute-start(bf16[1024,128]{1,0:T(8,128)(2,1)} %t0.1), channel_id=1, source_target_pairs={{0,2},{1,3},{2,0},{3,1},{4,6},{5,7},{6,4},{7,5},{8,10},{9,11},{10,... | collective-permute-start | bytes 786440 | tf_op jit(solution)/shard_map/ppermute | solution.py:234
  4.2 1.0 %copy-done = f32[1024,128]{1,0:T(8,128)S(1)} copy-done((f32[1024,128]{1,0:T(8,128)S(1)}, f32[1024,128]{1,0:T(8,128)}, u32[]{:S(2)}) %copy-start) | copy-done | bytes 524312
  5.3 0.2 shard_map.145.taps
  5.5 0.0 copy-start.1
  5.5 0.0 collective-permute-done.1.t1
  5.6 0.6 copy-done.14
  6.2 0.4 collective-permute-start.2
  6.6 0.7 copy-done.3
  7.3 0.1 dynamic-slice_bitcast_fusion
  7.4 0.1 copy.24
  7.5 3.5 %collective-permute-done.t2 = bf16[1024,128]{1,0:T(8,128)(2,1)S(1)} collective-permute-done((bf16[1024,128]{1,0:T(8,128)(2,1)}, bf16[1024,128]{1,0:T(8,128)(2,1)S(1)}, u32[]{:S(2)}, u32[]{:S(2)}) %collective-permute-start) | collective-permute-done | bytes 262176 | tf_op jit(solution)/shard_map/ppermute | solution.py:234
  11.0 0.0 collective-permute-done.2.w1
  11.0 0.9 %collective-permute-start.3 = (bf16[1024,128]{1,0:T(8,128)(2,1)S(1)}, bf16[1024,128]{1,0:T(8,128)(2,1)S(1)}, u32[]{:S(2)}, u32[]{:S(2)}) collective-permute-start(bf16[1024,128]{1,0:T(8,128)(2,1)S(1)} %collective-permute-done.t2), channel_id=1, source_target_pairs={{0,1},{1,0},{2,3},{3,2},{4,5},{5,4},{6,7},{7,6},{8,9},{9,8},{10,11... | collective-permute-start | bytes 786440 | tf_op jit(solution)/shard_map/ppermute | solution.py:234
  11.9 0.1 pad_add_fusion.me
  12.0 1.1 %collective-permute-done.3.t3 = bf16[1024,128]{1,0:T(8,128)(2,1)S(1)} collective-permute-done((bf16[1024,128]{1,0:T(8,128)(2,1)S(1)}, bf16[1024,128]{1,0:T(8,128)(2,1)S(1)}, u32[]{:S(2)}, u32[]{:S(2)}) %collective-permute-start.3) | collective-permute-done | bytes 262176 | tf_op jit(solution)/shard_map/ppermute | solution.py:234
  13.1 0.0 copy-done.2
  13.1 0.0 copy-done.1
  13.1 0.0 copy-done.4
  13.1 0.0 copy-start.11
  13.1 0.0 copy-start.12
  13.1 0.0 copy-start.13
  13.1 1.7 %shard_map.146 = (bf16[32,72,128]{2,1,0:T(8,128)(2,1)S(1)}, f32[1024,128]{1,0:T(8,128)S(1)}, f32[1024,128]{1,0:T(8,128)S(1)}, f32[16,128]{1,0:T(8,128)S(1)}) custom-call(s32[2]{0:T(128)S(1)} %pad_add_fusion.me, bf16[1024,128]{1,0:T(8,128)(2,1)S(1)} %copy-done.2, bf16[1024,128]{1,0:T(8,128)(2,1)S(1)} %collective-permute-done.1.t1, ...), custom_call_target="tpu_custom_call" | custom-call | flops 419430400 | bytes 1709064 | tf_op jit(solution)/shard_map/pallas_call | solution.py:222
  14.8 0.0 copy-start.5
  14.9 0.0 copy-start.6
  14.9 0.0 copy-start.7
  14.9 0.0 copy-start.8
  14.9 0.0 copy-start.10
  14.9 19.9 %all_to_all.10.sig = bf16[32,72,128]{2,1,0:T(8,128)(2,1)S(1)} all-to-all(bf16[32,72,128]{2,1,0:T(8,128)(2,1)S(1)} %get-tuple-element.31), channel_id=1, replica_groups=mesh['seq'=32,'chan'=4] {'seq'}, dimensions={0} | all-to-all | bytes 1179648 | tf_op jit(solution)/shard_map/all_to_all | solution.py:282
  34.8 0.0 copy-done.9
  34.8 0.0 copy-done.11
  34.8 0.0 copy-done.12
  34.8 0.0 copy-done.13
  34.8 0.0 copy-done.5
  34.9 3.3 %shard_map.147 = bf16[32,40,128]{2,1,0:T(8,128)(2,1)S(1)} custom-call(bf16[32,72,128]{2,1,0:T(8,128)(2,1)S(1)} %all_to_all.10.sig, f32[128,128]{1,0:T(8,128)S(1)} %bitcast.12, f32[256,256]{1,0:T(8,128)S(1)} %copy-done.9, bf16[512,256]{1,0:T(8,128)(2,1)S(1)} %copy-done.8, bf16[512,256]{1,0:T(8,128)(2,1)S(1)} %copy-done.7, bf16[256,256]{1,0:T(8,128)(2,1)S(1)} %copy-done.13, ...), custom_call_target="tpu_custom_call" | custom-call | flops 2222981120 | bytes 2490368 | tf_op jit(solution)/shard_map/pallas_call | solution.py:222
  38.2 13.6 %all_to_all.11.conv = bf16[32,40,128]{2,1,0:T(8,128)(2,1)S(1)} all-to-all(bf16[32,40,128]{2,1,0:T(8,128)(2,1)S(1)} %shard_map.147), channel_id=1, replica_groups=mesh['seq'=32,'chan'=4] {'seq'}, dimensions={0} | all-to-all | bytes 655360 | tf_op jit(solution)/shard_map/all_to_all | solution.py:291
  51.8 0.3 shard_map.148.g0
  52.0 2.5 %collective-permute-start.5 = (bf16[1024,128]{1,0:T(8,128)(2,1)S(1)}, bf16[1024,128]{1,0:T(8,128)(2,1)S(1)}, u32[]{:S(2)}, u32[]{:S(2)}) collective-permute-start(bf16[1024,128]{1,0:T(8,128)(2,1)S(1)} %shard_map.148.g0), channel_id=1, source_target_pairs={{0,1},{1,0},{2,3},{3,2},{4,5},{5,4},{6,7},{7,6},{8,9},{9,8},{10,11... | collective-permute-start | bytes 786440 | tf_op jit(solution)/shard_map/ppermute | solution.py:234
  54.6 2.4 %collective-permute-start.4 = (bf16[256,128]{1,0:T(8,128)(2,1)S(1)}, bf16[256,128]{1,0:T(8,128)(2,1)S(1)}, u32[]{:S(2)}, u32[]{:S(2)}) collective-permute-start(bf16[256,128]{1,0:T(8,128)(2,1)S(1)} %pad_maximum_fusion), channel_id=1, source_target_pairs={{0,2},{1,3},{2,0},{3,1},{4,6},{5,7},{6,4},{7,5},{8,10},{9,11},{10,... | collective-permute-start | bytes 196616 | tf_op jit(solution)/shard_map/ppermute | solution.py:234
  57.0 0.5 collective-permute-start.6
  57.5 2.1 %collective-permute-done.4 = bf16[256,128]{1,0:T(8,128)(2,1)S(1)} collective-permute-done((bf16[256,128]{1,0:T(8,128)(2,1)S(1)}, bf16[256,128]{1,0:T(8,128)(2,1)S(1)}, u32[]{:S(2)}, u32[]{:S(2)}) %collective-permute-start.4) | collective-permute-done | bytes 65568 | tf_op jit(solution)/shard_map/ppermute | solution.py:234
  59.6 0.0 collective-permute-done.5.g1
  59.6 1.0 %collective-permute-start.7 = (bf16[128,128]{1,0:T(8,128)(2,1)S(1)}, bf16[128,128]{1,0:T(8,128)(2,1)S(1)}, u32[]{:S(2)}, u32[]{:S(2)}) collective-permute-start(bf16[128,128]{1,0:T(8,128)(2,1)S(1)} %get-tuple-element.48), channel_id=1, source_target_pairs={{0,1},{1,0},{2,3},{3,2},{4,5},{5,4},{6,7},{7,6},{8,9},{9,8},{10,11... | collective-permute-start | bytes 98312 | tf_op jit(solution)/shard_map/ppermute | solution.py:234
  60.7 5.3 %collective-permute-done.6.g2 = bf16[1024,128]{1,0:T(8,128)(2,1)S(1)} collective-permute-done((bf16[1024,128]{1,0:T(8,128)(2,1)S(1)}, bf16[1024,128]{1,0:T(8,128)(2,1)S(1)}, u32[]{:S(2)}, u32[]{:S(2)}) %collective-permute-start.6) | collective-permute-done | bytes 262176 | tf_op jit(solution)/shard_map/ppermute | solution.py:234
  66.0 0.0 collective-permute-done.7.w3
  66.0 1.2 %collective-permute-start.8 = (bf16[1024,128]{1,0:T(8,128)(2,1)S(1)}, bf16[1024,128]{1,0:T(8,128)(2,1)S(1)}, u32[]{:S(2)}, u32[]{:S(2)}) collective-permute-start(bf16[1024,128]{1,0:T(8,128)(2,1)S(1)} %collective-permute-done.6.g2), channel_id=1, source_target_pairs={{0,1},{1,0},{2,3},{3,2},{4,5},{5,4},{6,7},{7,6},{8,9},{9,8},{10,11... | collective-permute-start | bytes 786440 | tf_op jit(solution)/shard_map/ppermute | solution.py:234
  67.2 1.2 %collective-permute-done.8.g3 = bf16[1024,128]{1,0:T(8,128)(2,1)S(1)} collective-permute-done((bf16[1024,128]{1,0:T(8,128)(2,1)S(1)}, bf16[1024,128]{1,0:T(8,128)(2,1)S(1)}, u32[]{:S(2)}, u32[]{:S(2)}) %collective-permute-start.8) | collective-permute-done | bytes 262176 | tf_op jit(solution)/shard_map/ppermute | solution.py:234
  68.4 1.1 %shard_map.149 = bf16[1024,128]{1,0:T(8,128)(2,1)} custom-call(bf16[1024,128]{1,0:T(8,128)(2,1)S(1)} %shard_map.148.g0, bf16[1024,128]{1,0:T(8,128)(2,1)S(1)} %collective-permute-done.5.g1, bf16[1024,128]{1,0:T(8,128)(2,1)S(1)} %collective-permute-done.6.g2, bf16[1024,128]{1,0:T(8,128)(2,1)S(1)} %collective-permute-done.8.g3, ...), custom_call_target="tpu_custom_call" | custom-call | flops 134217728 | bytes 1179648 | tf_op jit(solution)/shard_map/pallas_call | solution.py:222
  (19 shorter events, 0.1 us)
Async XLA Ops:
  0.0 5.5 %collective-permute-start.1 = (bf16[1024,128]{1,0:T(8,128)(2,1)}, bf16[1024,128]{1,0:T(8,128)(2,1)S(1)}, u32[]{:S(2)}, u32[]{:S(2)}) collective-permute-start(bf16[1024,128]{1,0:T(8,128)(2,1)} %t0.1), channel_id=1, source_target_pairs={{0,1},{1,0},{2,3},{3,2},{4,5},{5,4},{6,7},{7,6},{8,9},{9,8},{10,11... | collective-permute-start | bytes 786440 | tf_op jit(solution)/shard_map/ppermute | solution.py:234
  1.4 9.6 %collective-permute-start = (bf16[1024,128]{1,0:T(8,128)(2,1)}, bf16[1024,128]{1,0:T(8,128)(2,1)S(1)}, u32[]{:S(2)}, u32[]{:S(2)}) collective-permute-start(bf16[1024,128]{1,0:T(8,128)(2,1)} %t0.1), channel_id=1, source_target_pairs={{0,2},{1,3},{2,0},{3,1},{4,6},{5,7},{6,4},{7,5},{8,10},{9,11},{10,... | collective-permute-start | bytes 786440 | tf_op jit(solution)/shard_map/ppermute | solution.py:234
  4.2 1.0 %copy-start = (f32[1024,128]{1,0:T(8,128)S(1)}, f32[1024,128]{1,0:T(8,128)}, u32[]{:S(2)}) copy-start(f32[1024,128]{1,0:T(8,128)} %value.1) | copy-start | bytes 1572868
  5.3 0.9 %copy-start.14 = (bf16[128,512]{1,0:T(8,128)(2,1)S(1)}, bf16[128,512]{1,0:T(8,128)(2,1)}, u32[]{:S(2)}) copy-start(bf16[128,512]{1,0:T(8,128)(2,1)} %param.20) | copy-start | bytes 393220
  5.3 7.8 %copy-start.2 = (bf16[1024,128]{1,0:T(8,128)(2,1)S(1)}, bf16[1024,128]{1,0:T(8,128)(2,1)}, u32[]{:S(2)}) copy-start(bf16[1024,128]{1,0:T(8,128)(2,1)} %t0.1) | copy-start | bytes 786436
  5.5 7.6 %copy-start.1 = (bf16[512,3,128]{2,0,1:T(8,128)(2,1)S(1)}, bf16[512,3,128]{2,0,1:T(8,128)(2,1)}, u32[]{:S(2)}) copy-start(bf16[512,3,128]{2,0,1:T(8,128)(2,1)} %param.16) | copy-start | bytes 1179652
  6.2 4.7 %collective-permute-start.2 = (bf16[128,128]{1,0:T(8,128)(2,1)S(1)}, bf16[128,128]{1,0:T(8,128)(2,1)S(1)}, u32[]{:S(2)}, u32[]{:S(2)}) collective-permute-start(bf16[128,128]{1,0:T(8,128)(2,1)S(1)} %get-tuple-element.45), channel_id=1, source_target_pairs={{0,1},{1,0},{2,3},{3,2},{4,5},{5,4},{6,7},{7,6},{8,9},{9,8},{10,11... | collective-permute-start | bytes 98312 | tf_op jit(solution)/shard_map/ppermute | solution.py:234
  6.6 0.7 copy-start.3
  11.0 2.1 %collective-permute-start.3 = (bf16[1024,128]{1,0:T(8,128)(2,1)S(1)}, bf16[1024,128]{1,0:T(8,128)(2,1)S(1)}, u32[]{:S(2)}, u32[]{:S(2)}) collective-permute-start(bf16[1024,128]{1,0:T(8,128)(2,1)S(1)} %collective-permute-done.t2), channel_id=1, source_target_pairs={{0,1},{1,0},{2,3},{3,2},{4,5},{5,4},{6,7},{7,6},{8,9},{9,8},{10,11... | collective-permute-start | bytes 786440 | tf_op jit(solution)/shard_map/ppermute | solution.py:234
  12.0 1.1 %copy-start.4 = (f32[128]{0:T(128)S(1)}, f32[128]{0:T(128)}, u32[]{:S(2)}) copy-start(f32[128]{0:T(128)} %param.19) | copy-start | bytes 1540
  13.1 21.7 %copy-start.9 = (f32[256,256]{1,0:T(8,128)S(1)}, f32[256,256]{1,0:T(8,128)}, u32[]{:S(2)}) copy-start(f32[256,256]{1,0:T(8,128)} %constant.43.clone.tw) | copy-start | bytes 786436
  13.1 21.7 %copy-start.11 = (bf16[256,256]{1,0:T(8,128)(2,1)S(1)}, bf16[256,256]{1,0:T(8,128)(2,1)}, u32[]{:S(2)}) copy-start(bf16[256,256]{1,0:T(8,128)(2,1)} %constant.48.clone.t_hi) | copy-start | bytes 393220
  13.1 21.7 %copy-start.12 = (bf16[256,256]{1,0:T(8,128)(2,1)S(1)}, bf16[256,256]{1,0:T(8,128)(2,1)}, u32[]{:S(2)}) copy-start(bf16[256,256]{1,0:T(8,128)(2,1)} %constant.47.clone.s_lo) | copy-start | bytes 393220
  13.1 21.7 %copy-start.13 = (bf16[256,256]{1,0:T(8,128)(2,1)S(1)}, bf16[256,256]{1,0:T(8,128)(2,1)}, u32[]{:S(2)}) copy-start(bf16[256,256]{1,0:T(8,128)(2,1)} %constant.46.clone.s_hi) | copy-start | bytes 393220
  14.8 20.0 %copy-start.5 = (bf16[256,512]{1,0:T(8,128)(2,1)S(1)}, bf16[256,512]{1,0:T(8,128)(2,1)}, u32[]{:S(2)}) copy-start(bf16[256,512]{1,0:T(8,128)(2,1)} %constant.51.clone.l_lo) | copy-start | bytes 786436
  14.9 20.0 %copy-start.6 = (bf16[256,512]{1,0:T(8,128)(2,1)S(1)}, bf16[256,512]{1,0:T(8,128)(2,1)}, u32[]{:S(2)}) copy-start(bf16[256,512]{1,0:T(8,128)(2,1)} %constant.50.clone.l_hi) | copy-start | bytes 786436
  14.9 20.0 %copy-start.7 = (bf16[512,256]{1,0:T(8,128)(2,1)S(1)}, bf16[512,256]{1,0:T(8,128)(2,1)}, u32[]{:S(2)}) copy-start(bf16[512,256]{1,0:T(8,128)(2,1)} %constant.45.clone.f_lo) | copy-start | bytes 786436
  14.9 20.0 %copy-start.8 = (bf16[512,256]{1,0:T(8,128)(2,1)S(1)}, bf16[512,256]{1,0:T(8,128)(2,1)}, u32[]{:S(2)}) copy-start(bf16[512,256]{1,0:T(8,128)(2,1)} %constant.44.clone.f_hi) | copy-start | bytes 786436
  14.9 20.0 %copy-start.10 = (bf16[256,256]{1,0:T(8,128)(2,1)S(1)}, bf16[256,256]{1,0:T(8,128)(2,1)}, u32[]{:S(2)}) copy-start(bf16[256,256]{1,0:T(8,128)(2,1)} %constant.49.clone.t_lo) | copy-start | bytes 393220
  52.0 7.6 %collective-permute-start.5 = (bf16[1024,128]{1,0:T(8,128)(2,1)S(1)}, bf16[1024,128]{1,0:T(8,128)(2,1)S(1)}, u32[]{:S(2)}, u32[]{:S(2)}) collective-permute-start(bf16[1024,128]{1,0:T(8,128)(2,1)S(1)} %shard_map.148.g0), channel_id=1, source_target_pairs={{0,1},{1,0},{2,3},{3,2},{4,5},{5,4},{6,7},{7,6},{8,9},{9,8},{10,11... | collective-permute-start | bytes 786440 | tf_op jit(solution)/shard_map/ppermute | solution.py:234
  54.6 5.1 %collective-permute-start.4 = (bf16[256,128]{1,0:T(8,128)(2,1)S(1)}, bf16[256,128]{1,0:T(8,128)(2,1)S(1)}, u32[]{:S(2)}, u32[]{:S(2)}) collective-permute-start(bf16[256,128]{1,0:T(8,128)(2,1)S(1)} %pad_maximum_fusion), channel_id=1, source_target_pairs={{0,2},{1,3},{2,0},{3,1},{4,6},{5,7},{6,4},{7,5},{8,10},{9,11},{10,... | collective-permute-start | bytes 196616 | tf_op jit(solution)/shard_map/ppermute | solution.py:234
  57.0 9.0 %collective-permute-start.6 = (bf16[1024,128]{1,0:T(8,128)(2,1)S(1)}, bf16[1024,128]{1,0:T(8,128)(2,1)S(1)}, u32[]{:S(2)}, u32[]{:S(2)}) collective-permute-start(bf16[1024,128]{1,0:T(8,128)(2,1)S(1)} %shard_map.148.g0), channel_id=1, source_target_pairs={{0,2},{1,3},{2,0},{3,1},{4,6},{5,7},{6,4},{7,5},{8,10},{9,11},{10,... | collective-permute-start | bytes 786440 | tf_op jit(solution)/shard_map/ppermute | solution.py:234
  59.6 6.4 %collective-permute-start.7 = (bf16[128,128]{1,0:T(8,128)(2,1)S(1)}, bf16[128,128]{1,0:T(8,128)(2,1)S(1)}, u32[]{:S(2)}, u32[]{:S(2)}) collective-permute-start(bf16[128,128]{1,0:T(8,128)(2,1)S(1)} %get-tuple-element.48), channel_id=1, source_target_pairs={{0,1},{1,0},{2,3},{3,2},{4,5},{5,4},{6,7},{7,6},{8,9},{9,8},{10,11... | collective-permute-start | bytes 98312 | tf_op jit(solution)/shard_map/ppermute | solution.py:234
  66.0 2.4 %collective-permute-start.8 = (bf16[1024,128]{1,0:T(8,128)(2,1)S(1)}, bf16[1024,128]{1,0:T(8,128)(2,1)S(1)}, u32[]{:S(2)}, u32[]{:S(2)}) collective-permute-start(bf16[1024,128]{1,0:T(8,128)(2,1)S(1)} %collective-permute-done.6.g2), channel_id=1, source_target_pairs={{0,1},{1,0},{2,3},{3,2},{4,5},{5,4},{6,7},{7,6},{8,9},{9,8},{10,11... | collective-permute-start | bytes 786440 | tf_op jit(solution)/shard_map/ppermute | solution.py:234
